TPU v7x, 128 devices: a whole 4x4x4 slice. The times are simulated.
128 devices in a mesh: seq: 32 (over x, z_lo, y), head: 2 (over core), dp: 2 (over z_hi).
Axes of the slice: x: 4, y: 4, z: 4 (z_hi: 2, z_lo: 2; z = z_hi * 2 + z_lo), core: 2. Of those that a mesh axis runs over, the one named last changes fastest.
Arguments:
- queries: bfloat16 [16384, 2048], P(('dp', 'seq'), 'head'), parts along dimension 0, may hold values from -32 to 32
- keys: bfloat16 [16384, 2048], P(('dp', 'seq'), 'head'), parts along dimension 0, may hold values from -32 to 32
- values: bfloat16 [16384, 2048], P(('dp', 'seq'), 'head'), parts along dimension 0, may hold values from -6 to 6
- out_grad: bfloat16 [16384, 4096], P(('dp', 'seq')), parts along dimension 0, may hold values from -6 to 6
- proj_weight: bfloat16 [4096, 2048], P(None, 'head'), may hold values from -0.09375 to 0.09375
- layout: int32 [64, 12], replicated, may hold values from -1 to 63, as said below
Outputs:
- query_grad: bfloat16 [16384, 2048], P(('dp', 'seq'), 'head'), parts along dimension 0
- key_grad: bfloat16 [16384, 2048], P(('dp', 'seq'), 'head'), parts along dimension 0
- value_grad: bfloat16 [16384, 2048], P(('dp', 'seq'), 'head'), parts along dimension 0
- proj_grad: float32 [8192, 2048], P(('dp', 'seq'), 'head'), parts along dimension 0
There are 2 independent parts, one for each index of `dp`. A program takes and returns all parts, laid end to end along the dimension named above; an argument that names none is the same for every part. Nothing has to cross between parts.
Inputs may be any that keep to these rules, and one draw needn't show every extreme that they name: `layout`: row i lists, in increasing order, some of the blocks j < i - 7 whose remainder modulo 16 equals one offset, below 8 and shared by all rows (the last row lists all of them), then the blocks max(0, i - w + 1) to i for a window w of its own between 1 and 8, and ends with -1 in the unused entries; a row whose block follows a block of that remainder has w = 8.
All inputs are finite; a program needn't handle non-finite values.
Results may differ from a plain program's by a relative error of at most 0.03.
Values may be sent and summed in bfloat16 or wider, within the bound.
A program may use at most 192 MiB of HBM per device.

v0:
```python
import jax
import jax.numpy as jnp
from jax import lax
from jax.sharding import PartitionSpec as P

HD = 128
BLK = 128
LOCAL = 8
STRIDE = 16


def passed_along(block, axis, distance):
    devices = range(lax.axis_size(axis))
    route = [(i - distance, i) for i in devices if i - distance in devices]
    return lax.ppermute(block, axis, route)


def listed(table_rows, block_ids):
    hit = jnp.any(table_rows[:, None, :] == block_ids[:, :, None], axis=2)
    return hit & (block_ids >= 0)


def local(queries, keys, values, out_grad, proj_weight, layout):
    tok_dev = queries.shape[0]
    width = queries.shape[1]
    heads_here = width // HD
    blocks_dev = tok_dev // BLK
    block_count = layout.shape[0]
    summary_count = block_count // STRIDE
    score_scale = HD ** (-0.5)
    me = lax.axis_index("seq")
    first_block = me * blocks_dev
    offset_block = layout[block_count - 1, 0] % STRIDE
    reach_back = (LOCAL - 2) // blocks_dev + 1
    span_blocks = [
        min(blocks_dev, LOCAL - 1 - hop_index * blocks_dev) for hop_index in range(reach_back)
    ]
    back_blocks = sum(span_blocks)
    pool_blocks = back_blocks + blocks_dev
    attn_grad = jnp.dot(out_grad, proj_weight, preferred_element_type=jnp.float32).astype(
        jnp.bfloat16
    )
    kv = jnp.concatenate([keys, values], axis=1)
    near = []
    for distance in range(reach_back, 0, -1):
        rows_needed = span_blocks[distance - 1] * BLK
        near.append(passed_along(kv[tok_dev - rows_needed :], "seq", distance))
    pool_kv = jnp.concatenate(near + [kv], axis=0)
    far_ids = jnp.arange(summary_count, dtype=jnp.int32) * STRIDE + offset_block
    far_owner = far_ids // blocks_dev
    far_local = far_ids % blocks_dev
    kv_blocks = kv.reshape(blocks_dev, BLK, 2 * width)
    far_mine = jnp.where(
        (far_owner == me)[:, None, None],
        jnp.take(kv_blocks, far_local, axis=0),
        jnp.zeros_like(kv_blocks[:1]),
    ).reshape(summary_count * BLK, 2 * width)
    far_part = lax.psum_scatter(far_mine, "seq", scatter_dimension=0, tiled=True)
    far_kv = lax.all_gather(far_part, "seq", axis=0, tiled=True)
    all_kv = jnp.concatenate([pool_kv, far_kv], axis=0)
    key_rows = all_kv[:, :width].reshape(-1, heads_here, HD)
    value_rows = all_kv[:, width:].reshape(-1, heads_here, HD)
    query_rows = queries.reshape(tok_dev, heads_here, HD)
    grad_rows = attn_grad.reshape(tok_dev, heads_here, HD)
    own_ids = first_block + jnp.arange(blocks_dev, dtype=jnp.int32)
    table_rows = lax.dynamic_slice_in_dim(layout, first_block, blocks_dev, 0)
    pool_ids = first_block - back_blocks + jnp.arange(pool_blocks, dtype=jnp.int32)
    pool_ids_b = jnp.broadcast_to(pool_ids[None, :], (blocks_dev, pool_blocks))
    plain = (pool_ids_b % STRIDE != offset_block) | (pool_ids_b == own_ids[:, None])
    pool_ok = listed(table_rows, pool_ids_b) & plain
    far_ids_b = jnp.broadcast_to(far_ids[None, :], (blocks_dev, summary_count))
    far_ok = listed(table_rows, far_ids_b) & (far_ids_b < own_ids[:, None])
    block_ok = jnp.concatenate([pool_ok, far_ok], axis=1)
    token_ok = jnp.repeat(jnp.repeat(block_ok, BLK, axis=0), BLK, axis=1)
    query_pos = jnp.arange(tok_dev, dtype=jnp.int32)
    pool_pos = jnp.arange(pool_blocks * BLK, dtype=jnp.int32) - back_blocks * BLK
    causal = jnp.concatenate(
        [
            pool_pos[None, :] <= query_pos[:, None],
            jnp.ones((tok_dev, summary_count * BLK), jnp.bool_),
        ],
        axis=1,
    )
    allowed = token_ok & causal
    scores = (
        jnp.einsum("qhd,khd->hqk", query_rows, key_rows, preferred_element_type=jnp.float32)
        * score_scale
    )
    scores = jnp.where(allowed[None], scores, -jnp.inf)
    row_top = jnp.max(scores, axis=-1, keepdims=True)
    log_total = row_top + jnp.log(jnp.sum(jnp.exp(scores - row_top), axis=-1, keepdims=True))
    probs = jnp.exp(scores - log_total)
    probs_low = probs.astype(jnp.bfloat16)
    attn_out = jnp.einsum(
        "hqk,khd->qhd", probs_low, value_rows, preferred_element_type=jnp.float32
    ).astype(jnp.bfloat16)
    delta = jnp.transpose(
        jnp.sum(attn_out.astype(jnp.float32) * grad_rows.astype(jnp.float32), axis=-1)
    )[..., None]
    dprobs = jnp.einsum("qhd,khd->hqk", grad_rows, value_rows, preferred_element_type=jnp.float32)
    dscores = (score_scale * probs * (dprobs - delta)).astype(jnp.bfloat16)
    query_grad = jnp.einsum(
        "hqk,khd->qhd", dscores, key_rows, preferred_element_type=jnp.float32
    ).astype(jnp.bfloat16)
    key_part = jnp.einsum("hqk,qhd->khd", dscores, query_rows, preferred_element_type=jnp.float32)
    value_part = jnp.einsum(
        "hqk,qhd->khd", probs_low, grad_rows, preferred_element_type=jnp.float32
    )
    grad_kv = jnp.concatenate([key_part.reshape(-1, width), value_part.reshape(-1, width)], axis=1)
    far_grad = grad_kv[pool_blocks * BLK :]
    far_sum = lax.all_gather(
        lax.psum_scatter(far_grad, "seq", scatter_dimension=0, tiled=True),
        "seq",
        axis=0,
        tiled=True,
    ).reshape(summary_count, BLK, 2 * width)
    is_summary = own_ids % STRIDE == offset_block
    summary_slot = jnp.minimum(own_ids // STRIDE, summary_count - 1)
    far_add = jnp.where(is_summary[:, None, None], jnp.take(far_sum, summary_slot, axis=0), 0.0)
    own_grad = grad_kv[back_blocks * BLK : pool_blocks * BLK]
    pool_start = 0
    for distance in range(reach_back, 0, -1):
        rows_needed = span_blocks[distance - 1] * BLK
        back = passed_along(grad_kv[pool_start : pool_start + rows_needed], "seq", -distance)
        own_grad = own_grad.at[tok_dev - rows_needed :].add(back)
        pool_start = pool_start + rows_needed
    total = own_grad.reshape(blocks_dev, BLK, 2 * width) + far_add
    total = total.reshape(tok_dev, 2 * width).astype(jnp.bfloat16)
    proj_grad = lax.psum_scatter(
        lax.dot_general(
            out_grad,
            attn_out.reshape(tok_dev, width),
            (((0,), (0,)), ((), ())),
            preferred_element_type=jnp.float32,
        ),
        "seq",
        scatter_dimension=0,
        tiled=True,
    )
    return (query_grad.reshape(tok_dev, width), total[:, :width], total[:, width:], proj_grad)


def solution(mesh):
    return jax.shard_map(
        local,
        mesh=mesh,
        in_specs=(
            P(("dp", "seq"), "head"),
            P(("dp", "seq"), "head"),
            P(("dp", "seq"), "head"),
            P(("dp", "seq"), None),
            P(None, "head"),
            P(),
        ),
        out_specs=(
            P(("dp", "seq"), "head"),
            P(("dp", "seq"), "head"),
            P(("dp", "seq"), "head"),
            P(("dp", "seq"), "head"),
        ),
        check_vma=False,
    )
```

profile of v0, /device:TPU:0, one launch (start us, length us, event | category | flops | bytes accessed | tf_op | source)
XLA Modules:
  0.0 1129.2 jit_solution(14929468038700556082)
XLA Ops:
  7.2 1.4 slice.99
  10.6 1.2 copy.95
  11.9 1.4 copy.96
  13.3 0.8 copy-done.5
  14.1 1.0 pad_maximum_fusion.1
  15.1 1.5 copy.97
  16.7 2.0 gather_fusion
  18.7 4.0 copy.98
  22.7 0.1 broadcast_bitcast_fusion.3
  22.9 3.1 select_select_fusion
  26.0 4.0 copy.127
  30.0 6.1 collective-permute-start.1
  36.1 4.9 collective-permute-start.2
  41.0 2.8 collective-permute-start.3
  43.8 0.8 fusion.13
  44.6 2.1 collective-permute-start
  46.8 179.5 %reduce-scatter.10.cloned.1.call-done = bf16[16,2048]{1,0:T(8,128)(2,1)} async-done(((bf16[512,2048]{1,0:T(8,128)(2,1)}), bf16[16,2048]{1,0:T(8,128)(2,1)}) %reduce-scatter.10.cloned.1.call-update) | async-done | bytes 65552 | tf_op jit(solution)/shard_map/reduce_scatter | solution.py:58
  226.4 0.1 copy.101
  226.5 0.2 compare_reduce_fusion.1
  226.7 0.2 compare_reduce_fusion
  227.0 6.5 convolution_convert_fusion.2
  233.5 0.1 pad_add_fusion
  233.6 0.1 copy.103
  233.7 0.1 broadcast_bitcast_fusion
  233.8 2.0 copy.129
  235.9 2.0 copy.130
  237.9 0.2 iota_compare_fusion
  238.2 0.9 bitcast_and_fusion
  239.1 1.9 constant_dynamic-update-slice_fusion.5
  241.0 2.3 constant_dynamic-update-slice_fusion.4
  243.4 2.3 constant_dynamic-update-slice_fusion.3
  245.7 2.3 constant_dynamic-update-slice_fusion.2
  248.0 1.1 constant_dynamic-update-slice_fusion.1
  249.2 128.6 %all-gather.3.cloned.1.call-done = bf16[512,2048]{1,0:T(8,128)(2,1)} async-done(((bf16[16,2048]{1,0:T(8,128)(2,1)}), bf16[512,2048]{1,0:T(8,128)(2,1)}) %all-gather.3.cloned.1.call-update) | async-done | bytes 2097168 | tf_op jit(solution)/shard_map/all_gather | solution.py:59
  377.8 3.9 copy.100
  381.7 3.1 constant_dynamic-update-slice_fusion
  384.8 5.3 fusion.23
  390.0 7.5 fusion.1
  397.5 7.8 exponential_reduce_fusion
  405.4 10.4 multiply_reduce_fusion
  415.8 5.8 fusion.20
  421.6 10.1 multiply_convert_fusion
  431.8 7.7 copy.117
  439.5 7.9 fusion.25
  447.3 7.7 copy.116
  455.0 4.7 pad_maximum_fusion
  459.8 168.7 %reduce-scatter.6.cloned.1.call-done = f32[16,2048]{1,0:T(8,128)} async-done(((f32[512,2048]{1,0:T(8,128)}), f32[16,2048]{1,0:T(8,128)}) %reduce-scatter.6.cloned.1.call-update) | async-done | bytes 131088 | tf_op jit(solution)/shard_map/reduce_scatter | solution.py:112
  628.6 8.1 convolution_bitcast_fusion
  636.7 6.1 fusion.4
  642.8 1.3 collective-permute-start.7
  644.1 1.3 collective-permute-start.6
  645.4 1.3 collective-permute-start.5
  646.7 2.4 fusion.12
  649.1 1.3 collective-permute-start.4
  650.6 4.1 convolution_convert_fusion
  654.7 1.0 copy.118
  655.7 18.4 %collective-permute-done.4 = f32[128,2048]{1,0:T(8,128)} collective-permute-done((f32[128,2048]{1,0:T(8,128)}, f32[128,2048]{1,0:T(8,128)}, u32[]{:S(2)}, u32[]{:S(2)}) %collective-permute-start.4) | collective-permute-done | bytes 1048608 | tf_op jit(solution)/shard_map/ppermute | solution.py:15
  674.1 2.6 fusion.11
  676.8 218.7 %all-gather.5.cloned.1.call-done = f32[512,2048]{1,0:T(8,128)} async-done(((f32[16,2048]{1,0:T(8,128)}), f32[512,2048]{1,0:T(8,128)}) %all-gather.5.cloned.1.call-update) | async-done | bytes 4194320 | tf_op jit(solution)/shard_map/all_gather | solution.py:111
  895.5 4.2 gather_fusion.1
  899.7 4.6 fusion.8
  904.3 1.0 fusion.24
  905.4 215.2 %reduce-scatter.8.cloned.1.call-done = f32[128,1024]{0,1:T(8,128)} async-done(((f32[4096,1024]{0,1:T(8,128)}), f32[128,1024]{0,1:T(8,128)}) %reduce-scatter.8.cloned.1.call-update) | async-done | bytes 524304 | tf_op jit(solution)/shard_map/reduce_scatter | solution.py:129
  1120.6 2.0 copy.119
  (73 shorter events, 1.0 us)
Async XLA Ops:
  7.2 219.9 %copy-start = (bf16[256,4096]{1,0:T(8,128)(2,1)S(1)}, bf16[256,4096]{1,0:T(8,128)(2,1)}, u32[]{:S(2)}) copy-start(bf16[256,4096]{1,0:T(8,128)(2,1)} %param.23) | copy-start | bytes 6291460
  7.2 219.1 %reduce-scatter.10.cloned.1.call-start = ((), (), s32[]{:S(2)}) async-start(), calls=%async_computation.7 | async-start | bytes 2162688 | tf_op jit(solution)/shard_map/reduce_scatter | solution.py:58
  11.8 1.5 copy-start.3
  13.3 0.8 copy-start.5
  18.7 25.1 %copy-start.4 = (bf16[256,1024]{0,1:T(8,128)(2,1)S(1)}, bf16[256,1024]{0,1:T(8,128)(2,1)}, u32[]{:S(2)}) copy-start(bf16[256,1024]{0,1:T(8,128)(2,1)} %copy-done.3) | copy-start | bytes 1572868
  18.7 25.1 %copy-start.6 = (bf16[256,1024]{0,1:T(8,128)(2,1)S(1)}, bf16[256,1024]{0,1:T(8,128)(2,1)}, u32[]{:S(2)}) copy-start(bf16[256,1024]{0,1:T(8,128)(2,1)} %copy-done.5) | copy-start | bytes 1572868
  22.7 24.0 %copy-start.12 = (s32[64,12]{0,1:T(8,128)S(1)}, s32[64,12]{0,1:T(8,128)}, u32[]{:S(2)}) copy-start(s32[64,12]{0,1:T(8,128)} %param.25) | copy-start | bytes 9220
  30.0 347.8 %all-gather.3.cloned.1.call-start = ((), (), s32[]{:S(2)}) async-start(), calls=%async_computation.3 | async-start | bytes 2162688 | tf_op jit(solution)/shard_map/all_gather | solution.py:59
  30.0 211.0 %collective-permute-start.1 = (bf16[256,2048]{0,1:T(8,128)(2,1)}, bf16[256,2048]{0,1:T(8,128)(2,1)}, u32[]{:S(2)}, u32[]{:S(2)}) collective-permute-start(bf16[256,2048]{0,1:T(8,128)(2,1)} %pad_maximum_fusion.1), channel_id=1, source_target_pairs={{0,12},{4,16},{8,20},{12,24},{16,28},{20,32},{24,36},{28,40},{32,4... | collective-permute-start | bytes 3145736 | tf_op jit(solution)/shard_map/ppermute | solution.py:15
  36.1 207.3 %collective-permute-start.2 = (bf16[256,2048]{0,1:T(8,128)(2,1)}, bf16[256,2048]{0,1:T(8,128)(2,1)}, u32[]{:S(2)}, u32[]{:S(2)}) collective-permute-start(bf16[256,2048]{0,1:T(8,128)(2,1)} %pad_maximum_fusion.1), channel_id=1, source_target_pairs={{0,8},{4,12},{8,16},{12,20},{16,24},{20,28},{24,32},{28,36},{32,40... | collective-permute-start | bytes 3145736 | tf_op jit(solution)/shard_map/ppermute | solution.py:15
  41.0 204.8 %collective-permute-start.3 = (bf16[256,2048]{0,1:T(8,128)(2,1)}, bf16[256,2048]{0,1:T(8,128)(2,1)}, u32[]{:S(2)}, u32[]{:S(2)}) collective-permute-start(bf16[256,2048]{0,1:T(8,128)(2,1)} %pad_maximum_fusion.1), channel_id=1, source_target_pairs={{0,4},{4,8},{8,12},{12,16},{16,20},{20,24},{24,28},{28,32},{32,36}... | collective-permute-start | bytes 3145736 | tf_op jit(solution)/shard_map/ppermute | solution.py:15
  44.6 194.5 %collective-permute-start = (bf16[128,2048]{0,1:T(8,128)(2,1)}, bf16[128,2048]{0,1:T(8,128)(2,1)}, u32[]{:S(2)}, u32[]{:S(2)}) collective-permute-start(bf16[128,2048]{0,1:T(8,128)(2,1)} %fusion.13), channel_id=1, source_target_pairs={{0,16},{4,20},{8,24},{12,28},{16,32},{20,36},{24,40},{28,44},{32,4... | collective-permute-start | bytes 1572872 | tf_op jit(solution)/shard_map/ppermute | solution.py:15
  226.3 402.2 %reduce-scatter.6.cloned.1.call-start = ((), (), s32[]{:S(2)}) async-start(), calls=%async_computation.4 | async-start | bytes 4325376 | tf_op jit(solution)/shard_map/reduce_scatter | solution.py:112
  384.8 5.3 copy-start.7
  384.8 5.3 copy-start.8
  390.0 7.5 copy-start.1
  397.5 18.2 %slice-start = ((s8[13631488]{0:T(1024)(128)(4,1)}), s8[4194304]{0:T(1024)(128)(4,1)S(1)}, s32[]{:S(2)}) async-start(s8[13631488]{0:T(1024)(128)(4,1)} %bitcast.82), calls=%async_computation.8 | async-start | bytes 8388608
  397.5 18.2 %slice-start.1 = ((s8[13631488]{0:T(1024)(128)(4,1)}), s8[1048576]{0:T(1024)(128)(4,1)S(1)}, s32[]{:S(2)}) async-start(s8[13631488]{0:T(1024)(128)(4,1)} %bitcast.82), calls=%async_computation.9 | async-start | bytes 2097152
  405.3 10.4 slice-start.2
  405.3 10.4 slice-start.3
  405.3 10.4 copy-start.10
  431.8 7.7 copy-start.9
  455.0 173.6 %copy-start.11 = (bf16[8,128,256]{2,1,0:T(8,128)(2,1)S(1)}, bf16[8,128,256]{2,1,0:T(8,128)(2,1)}, u32[]{:S(2)}) copy-start(bf16[8,128,256]{2,1,0:T(8,128)(2,1)} %get-tuple-element.107) | copy-start | bytes 1572868
  459.8 435.7 %all-gather.5.cloned.1.call-start = ((), (), s32[]{:S(2)}) async-start(), calls=%async_computation.5 | async-start | bytes 4325376 | tf_op jit(solution)/shard_map/all_gather | solution.py:111
  628.5 492.1 %reduce-scatter.8.cloned.1.call-start = ((), (), s32[]{:S(2)}) async-start(), calls=%async_computation.6 | async-start | bytes 17301504 | tf_op jit(solution)/shard_map/reduce_scatter | solution.py:129
  642.8 256.9 %collective-permute-start.7 = (f32[256,2048]{1,0:T(8,128)}, f32[256,2048]{1,0:T(8,128)}, u32[]{:S(2)}, u32[]{:S(2)}) collective-permute-start(f32[256,2048]{1,0:T(8,128)} %get-tuple-element.99), channel_id=1, source_target_pairs={{4,0},{8,4},{12,8},{16,12},{20,16},{24,20},{28,24},{32,28},{36,32}... | collective-permute-start | bytes 6291464 | tf_op jit(solution)/shard_map/ppermute | solution.py:15
  644.1 255.6 %collective-permute-start.6 = (f32[256,2048]{1,0:T(8,128)}, f32[256,2048]{1,0:T(8,128)}, u32[]{:S(2)}, u32[]{:S(2)}) collective-permute-start(f32[256,2048]{1,0:T(8,128)} %get-tuple-element.98), channel_id=1, source_target_pairs={{8,0},{12,4},{16,8},{20,12},{24,16},{28,20},{32,24},{36,28},{40,32... | collective-permute-start | bytes 6291464 | tf_op jit(solution)/shard_map/ppermute | solution.py:15
  645.4 254.3 %collective-permute-start.5 = (f32[256,2048]{1,0:T(8,128)}, f32[256,2048]{1,0:T(8,128)}, u32[]{:S(2)}, u32[]{:S(2)}) collective-permute-start(f32[256,2048]{1,0:T(8,128)} %get-tuple-element.96), channel_id=1, source_target_pairs={{12,0},{16,4},{20,8},{24,12},{28,16},{32,20},{36,24},{40,28},{44,3... | collective-permute-start | bytes 6291464 | tf_op jit(solution)/shard_map/ppermute | solution.py:15
  646.7 3.9 copy-start.2
  649.1 25.0 %collective-permute-start.4 = (f32[128,2048]{1,0:T(8,128)}, f32[128,2048]{1,0:T(8,128)}, u32[]{:S(2)}, u32[]{:S(2)}) collective-permute-start(f32[128,2048]{1,0:T(8,128)} %fusion.12), channel_id=1, source_target_pairs={{16,0},{20,4},{24,8},{28,12},{32,16},{36,20},{40,24},{44,28},{48,3... | collective-permute-start | bytes 3145736 | tf_op jit(solution)/shard_map/ppermute | solution.py:15
Sparse Core Ops, SparseCore 0:
  30.1 196.1 reduce-scatter.9
  228.0 149.6 all-gather.2
  459.9 168.5 reduce-scatter.5
  630.1 265.3 all-gather.4
  897.9 222.7 reduce-scatter.7
where the time goes:
time: 1130 us
  waiting for transfers between devices  929 us (82%)
  local copies, waits for them, and re-layouts  66 us (6%)
  matrix products  60.4 us (5%)
  other arithmetic  36.3 us (3%)
  starting transfers between devices  21.2 us (2%)
  between operations  16 us (1%)
    all_gather x1, waiting for transfers between devices, local(): lax.all_gather(lax.psum_scatter(far_grad, 'seq', scatter_dimension=0, til...  219 us
    reduce_scatter x1, waiting for transfers between devices, local(): lax.psum_scatter(lax.dot_general(out_grad, attn_out.reshape(tok_dev, widt...  215 us
    reduce_scatter x1, waiting for transfers between devices, local(): lax.psum_scatter(far_mine, 'seq', scatter_dimension=0, tiled=True)  180 us
    reduce_scatter x1, waiting for transfers between devices, local(): lax.psum_scatter(far_grad, 'seq', scatter_dimension=0, tiled=True)  169 us
    all_gather x1, waiting for transfers between devices, local(): far_kv = lax.all_gather(far_part, 'seq', axis=0, tiled=True)  129 us
  transfers between devices with their start and end apart: 13, of which 6 were waited for; matrix products, arithmetic and copies ran while one was open for 5% of the time, Pallas kernels for 0%

commit v1 on v0

--- a/solution.py
+++ b/solution.py
@@ -56,7 +56,9 @@
         jnp.zeros_like(kv_blocks[:1]),
     ).reshape(summary_count * BLK, 2 * width)
     far_part = lax.psum_scatter(far_mine, "seq", scatter_dimension=0, tiled=True)
-    far_kv = lax.all_gather(far_part, "seq", axis=0, tiled=True)
+    far_kv = jnp.concatenate(
+        lax.all_to_all(jnp.stack([far_part] * lax.axis_size("seq")), "seq", 0, 0), axis=0
+    )
     all_kv = jnp.concatenate([pool_kv, far_kv], axis=0)
     key_rows = all_kv[:, :width].reshape(-1, heads_here, HD)
     value_rows = all_kv[:, width:].reshape(-1, heads_here, HD)

time: 1130 us -> 1000 us (0.88)
  waiting for transfers between devices: 929 us -> 794 us
    all_gather x1 -> x0, waiting for transfers between devices: 129 us -> none  [local(): far_kv = lax.all_gather(far_part, 'seq', axis=0, tiled=True)]
  transfers between devices with their start and end apart: 13 -> 13, of which waited for: 6 -> 6; matrix products, arithmetic and copies ran while one was open for 5% -> 6% of each run, Pallas kernels for 0% -> 0%
where the time goes in v1:
time: 1000 us
  waiting for transfers between devices  794 us (79%)
  local copies, waits for them, and re-layouts  69 us (7%)
  matrix products  62.4 us (6%)
  other arithmetic  33.4 us (3%)
  starting transfers between devices  26 us (3%)
  between operations  16 us (2%)
    all_gather x1, waiting for transfers between devices, local(): lax.all_gather(lax.psum_scatter(far_grad, 'seq', scatter_dimension=0, til...  214 us
    reduce_scatter x1, waiting for transfers between devices, local(): lax.psum_scatter(lax.dot_general(out_grad, attn_out.reshape(tok_dev, widt...  213 us
    reduce_scatter x1, waiting for transfers between devices, local(): lax.psum_scatter(far_mine, 'seq', scatter_dimension=0, tiled=True)  175 us
    reduce_scatter x1, waiting for transfers between devices, local(): lax.psum_scatter(far_grad, 'seq', scatter_dimension=0, tiled=True)  170 us
    ppermute x8, starting transfers between devices, passed_along(): return lax.ppermute(block, axis, route)  21 us
  transfers between devices with their start and end apart: 13, of which 6 were waited for; matrix products, arithmetic and copies ran while one was open for 6% of the time, Pallas kernels for 0%

profile of v1, /device:TPU:0, one launch (start us, length us, event | category | flops | bytes accessed | tf_op | source)
XLA Modules:
  0.0 1000.4 jit_solution(1577455977665321503)
XLA Ops:
  7.2 1.4 slice.99
  10.6 1.1 constant_dynamic-update-slice_fusion.1
  11.9 1.1 constant_dynamic-update-slice_fusion
  13.0 2.0 gather_fusion
  15.0 3.2 fusion.9
  18.2 6.0 collective-permute-start.1
  24.2 4.9 collective-permute-start.2
  29.2 2.9 collective-permute-start.3
  32.0 0.8 slice.115
  32.9 2.1 collective-permute-start
  35.0 0.1 copy.90
  35.2 0.2 compare_reduce_fusion.1
  35.4 0.2 compare_reduce_fusion
  35.7 0.1 or_and_fusion
  35.7 6.5 convolution_convert_fusion.2
  42.3 0.1 pad_add_fusion
  42.3 0.1 copy.92
  42.5 174.8 %reduce-scatter.4.cloned.1.call-done = bf16[16,2048]{1,0:T(8,128)(2,1)} async-done(((bf16[512,2048]{1,0:T(8,128)(2,1)}), bf16[16,2048]{1,0:T(8,128)(2,1)}) %reduce-scatter.4.cloned.1.call-update) | async-done | bytes 65552 | tf_op jit(solution)/shard_map/reduce_scatter | solution.py:58
  217.3 2.4 stack.2
  219.7 4.8 all-to-all-start
  224.5 0.1 broadcast_bitcast_fusion
  224.7 2.0 copy.117
  226.7 2.0 copy.118
  228.7 0.2 iota_compare_fusion
  229.0 0.9 bitcast_and_fusion
  229.9 1.9 constant_dynamic-update-slice_fusion.7
  231.8 2.3 constant_dynamic-update-slice_fusion.6
  234.2 2.3 constant_dynamic-update-slice_fusion.5
  236.5 2.3 constant_dynamic-update-slice_fusion.4
  238.8 0.9 constant_dynamic-update-slice_fusion.3
  239.7 0.8 constant_dynamic-update-slice_fusion.8
  240.5 2.3 all-to-all-done
  242.8 3.2 constant_dynamic-update-slice_fusion.2
  246.0 6.7 fusion.23
  252.7 5.9 copy.89
  258.5 5.6 copy.95
  264.1 9.4 fusion.1
  273.5 7.8 exponential_reduce_fusion
  281.3 10.4 %multiply_reduce_fusion = (f32[256,8]{0,1:T(8,128)S(1)}, bf16[8,128,256]{2,1,0:T(8,128)(2,1)}) fusion(bf16[256,1024]{0,1:T(8,128)(2,1)} %copy.118, bf16[1664,8,128]{0,2,1:T(8,128)(2,1)} %bitcast.94, f32[8,1664,256]{2,1,0:T(8,128)} %get-tuple-element.105, f32[8,256]{1,0:T(8,128)S(1)} %log_add_fusion, pred[256,1664]{0,1:T(8,128)(4,1)S(1)} %copy-done.2), kind=kOutput, calls=%fused_computation.41 | convolution fusion | flops 887355392 | bytes 18530304 | tf_op jit(solution)/shard_map/hqk,khd->qhd/dot_general | solution.py:96
  291.8 5.8 fusion.20
  297.6 10.1 %multiply_convert_fusion = bf16[8,256,1664]{1,2,0:T(8,128)(2,1)} fusion(f32[8,1664,256]{2,1,0:T(8,128)S(1)} %bitcast.86, f32[8,256]{1,0:T(8,128)S(1)} %bitcast.103, f32[8,256]{1,0:T(8,128)S(1)} %log_add_fusion, pred[256,1664]{0,1:T(8,128)(4,1)S(1)} %copy-done.2, bf16[256,8,128]{0,2,1:T(8,128)(2,1)} %bitcast.97, bf16[1664,8,128]{0,2,1:T(8,128)(2,1)} %bitcast.95), kind=kOutput, calls=%fused_computation.15 | convolution fusion | flops 896270336 | bytes 24821760 | tf_op jit(solution)/shard_map/qhd,khd->hqk/dot_general | solution.py:102
  307.7 7.7 copy.107
  315.4 7.9 fusion.25
  323.3 7.7 copy.106
  331.0 4.7 pad_maximum_fusion
  335.8 169.5 %reduce-scatter.6.cloned.1.call-done = f32[16,2048]{1,0:T(8,128)} async-done(((f32[512,2048]{1,0:T(8,128)}), f32[16,2048]{1,0:T(8,128)}) %reduce-scatter.6.cloned.1.call-update) | async-done | bytes 131088 | tf_op jit(solution)/shard_map/reduce_scatter | solution.py:114
  505.4 8.1 convolution_bitcast_fusion
  513.5 6.1 fusion.4
  519.6 1.3 collective-permute-start.7
  520.9 1.3 collective-permute-start.6
  522.2 1.3 collective-permute-start.5
  523.5 2.4 fusion.13
  525.9 1.3 collective-permute-start.4
  527.3 0.1 broadcast_bitcast_fusion.1
  527.3 4.1 convolution_convert_fusion
  531.4 1.0 copy.108
  532.4 19.3 %collective-permute-done.4 = f32[128,2048]{1,0:T(8,128)} collective-permute-done((f32[128,2048]{1,0:T(8,128)}, f32[128,2048]{1,0:T(8,128)}, u32[]{:S(2)}, u32[]{:S(2)}) %collective-permute-start.4) | collective-permute-done | bytes 1048608 | tf_op jit(solution)/shard_map/ppermute | solution.py:15
  551.8 2.6 fusion.12
  554.4 214.2 %all-gather.2.cloned.1.call-done = f32[512,2048]{1,0:T(8,128)} async-done(((f32[16,2048]{1,0:T(8,128)}), f32[512,2048]{1,0:T(8,128)}) %all-gather.2.cloned.1.call-update) | async-done | bytes 4194320 | tf_op jit(solution)/shard_map/all_gather | solution.py:113
  768.6 4.2 gather_fusion.1
  772.8 4.6 fusion.8
  777.4 1.0 fusion.24
  778.5 213.4 %reduce-scatter.8.cloned.1.call-done = f32[128,1024]{0,1:T(8,128)} async-done(((f32[4096,1024]{0,1:T(8,128)}), f32[128,1024]{0,1:T(8,128)}) %reduce-scatter.8.cloned.1.call-update) | async-done | bytes 524304 | tf_op jit(solution)/shard_map/reduce_scatter | solution.py:131
  991.8 2.0 copy.109
  (65 shorter events, 0.8 us)
Async XLA Ops:
  7.2 28.6 %copy-start = (bf16[256,4096]{1,0:T(8,128)(2,1)S(1)}, bf16[256,4096]{1,0:T(8,128)(2,1)}, u32[]{:S(2)}) copy-start(bf16[256,4096]{1,0:T(8,128)(2,1)} %param.23) | copy-start | bytes 6291460
  7.2 210.1 %reduce-scatter.4.cloned.1.call-start = ((), (), s32[]{:S(2)}) async-start(), calls=%async_computation.4 | async-start | bytes 2162688 | tf_op jit(solution)/shard_map/reduce_scatter | solution.py:58
  10.6 24.4 %copy-start.9 = (s32[64,12]{0,1:T(8,128)S(1)}, s32[64,12]{0,1:T(8,128)}, u32[]{:S(2)}) copy-start(s32[64,12]{0,1:T(8,128)} %param.25) | copy-start | bytes 9220
  18.2 213.6 %collective-permute-start.1 = (bf16[256,2048]{1,0:T(8,128)(2,1)S(1)}, bf16[256,2048]{1,0:T(8,128)(2,1)}, u32[]{:S(2)}, u32[]{:S(2)}) collective-permute-start(bf16[256,2048]{1,0:T(8,128)(2,1)S(1)} %constant_dynamic-update-slice_fusion), channel_id=1, source_target_pairs={{0,12},{4,16},{8,20},{12,24},{16,28},{20,32},{24,36},{28,40},{32,4... | collective-permute-start | bytes 3145736 | tf_op jit(solution)/shard_map/ppermute | solution.py:15
  24.2 209.9 %collective-permute-start.2 = (bf16[256,2048]{1,0:T(8,128)(2,1)S(1)}, bf16[256,2048]{1,0:T(8,128)(2,1)}, u32[]{:S(2)}, u32[]{:S(2)}) collective-permute-start(bf16[256,2048]{1,0:T(8,128)(2,1)S(1)} %constant_dynamic-update-slice_fusion), channel_id=1, source_target_pairs={{0,8},{4,12},{8,16},{12,20},{16,24},{20,28},{24,32},{28,36},{32,40... | collective-permute-start | bytes 3145736 | tf_op jit(solution)/shard_map/ppermute | solution.py:15
  29.2 207.3 %collective-permute-start.3 = (bf16[256,2048]{1,0:T(8,128)(2,1)S(1)}, bf16[256,2048]{1,0:T(8,128)(2,1)}, u32[]{:S(2)}, u32[]{:S(2)}) collective-permute-start(bf16[256,2048]{1,0:T(8,128)(2,1)S(1)} %constant_dynamic-update-slice_fusion), channel_id=1, source_target_pairs={{0,4},{4,8},{8,12},{12,16},{16,20},{20,24},{24,28},{28,32},{32,36}... | collective-permute-start | bytes 3145736 | tf_op jit(solution)/shard_map/ppermute | solution.py:15
  32.9 197.1 %collective-permute-start = (bf16[128,2048]{1,0:T(8,128)(2,1)}, bf16[128,2048]{1,0:T(8,128)(2,1)}, u32[]{:S(2)}, u32[]{:S(2)}) collective-permute-start(bf16[128,2048]{1,0:T(8,128)(2,1)} %slice.115), channel_id=1, source_target_pairs={{0,16},{4,20},{8,24},{12,28},{16,32},{20,36},{24,40},{28,44},{32,4... | collective-permute-start | bytes 1572872 | tf_op jit(solution)/shard_map/ppermute | solution.py:15
  219.7 23.1 %all-to-all-start = ((bf16[32,16,2048]{2,1,0:T(8,128)(2,1)}), bf16[32,16,2048]{2,1,0:T(8,128)(2,1)}, u32[]{:S(2)}, u32[]{:S(2)}) async-start(bf16[32,16,2048]{2,1,0:T(8,128)(2,1)} %stack.2), calls=%async_computation.1 | async-start | bytes 4194304 | tf_op jit(solution)/shard_map/all_to_all | solution.py:60
  224.5 280.8 %reduce-scatter.6.cloned.1.call-start = ((), (), s32[]{:S(2)}) async-start(), calls=%async_computation.5 | async-start | bytes 4325376 | tf_op jit(solution)/shard_map/reduce_scatter | solution.py:114
  228.7 10.1 %copy-start.6 = (bf16[256,1024]{1,0:T(8,128)(2,1)S(1)}, bf16[256,1024]{1,0:T(8,128)(2,1)}, u32[]{:S(2)}) copy-start(bf16[256,1024]{1,0:T(8,128)(2,1)} %param.21) | copy-start | bytes 1572868
  228.7 10.9 %copy-start.7 = (bf16[256,1024]{1,0:T(8,128)(2,1)S(1)}, bf16[256,1024]{1,0:T(8,128)(2,1)}, u32[]{:S(2)}) copy-start(bf16[256,1024]{1,0:T(8,128)(2,1)} %param.22) | copy-start | bytes 1572868
  252.7 11.4 %copy-start.2 = (pred[256,1664]{0,1:T(8,128)(4,1)S(1)}, pred[256,1664]{0,1:T(8,128)(4,1)}, u32[]{:S(2)}) copy-start(pred[256,1664]{0,1:T(8,128)(4,1)} %bitcast_and_fusion) | copy-start | bytes 1277956
  252.7 11.4 %copy-start.3 = (bf16[256,1024]{0,1:T(8,128)(2,1)S(1)}, bf16[256,1024]{0,1:T(8,128)(2,1)}, u32[]{:S(2)}) copy-start(bf16[256,1024]{0,1:T(8,128)(2,1)} %copy.117) | copy-start | bytes 1572868
  273.5 18.2 %slice-start = ((s8[13631488]{0:T(1024)(128)(4,1)}), s8[4194304]{0:T(1024)(128)(4,1)S(1)}, s32[]{:S(2)}) async-start(s8[13631488]{0:T(1024)(128)(4,1)} %bitcast.85), calls=%async_computation.8 | async-start | bytes 8388608
  273.5 18.2 %slice-start.1 = ((s8[13631488]{0:T(1024)(128)(4,1)}), s8[1048576]{0:T(1024)(128)(4,1)S(1)}, s32[]{:S(2)}) async-start(s8[13631488]{0:T(1024)(128)(4,1)} %bitcast.85), calls=%async_computation.9 | async-start | bytes 2097152
  281.3 10.4 %slice-start.2 = ((s8[13631488]{0:T(1024)(128)(4,1)}), s8[4194304]{0:T(1024)(128)(4,1)S(1)}, s32[]{:S(2)}) async-start(s8[13631488]{0:T(1024)(128)(4,1)} %bitcast.85), calls=%async_computation.10 | async-start | bytes 8388608
  281.3 10.4 %slice-start.3 = ((s8[13631488]{0:T(1024)(128)(4,1)}), s8[4194304]{0:T(1024)(128)(4,1)S(1)}, s32[]{:S(2)}) async-start(s8[13631488]{0:T(1024)(128)(4,1)} %bitcast.85), calls=%async_computation.11 | async-start | bytes 8388608
  281.3 10.4 %copy-start.5 = (bf16[256,1024]{0,1:T(8,128)(2,1)S(1)}, bf16[256,1024]{0,1:T(8,128)(2,1)}, u32[]{:S(2)}) copy-start(bf16[256,1024]{0,1:T(8,128)(2,1)} %copy.118) | copy-start | bytes 1572868
  307.7 7.7 copy-start.4
  331.0 174.4 %copy-start.8 = (bf16[8,128,256]{2,1,0:T(8,128)(2,1)S(1)}, bf16[8,128,256]{2,1,0:T(8,128)(2,1)}, u32[]{:S(2)}) copy-start(bf16[8,128,256]{2,1,0:T(8,128)(2,1)} %get-tuple-element.107) | copy-start | bytes 1572868
  335.7 432.8 %all-gather.2.cloned.1.call-start = ((), (), s32[]{:S(2)}) async-start(), calls=%async_computation.6 | async-start | bytes 4325376 | tf_op jit(solution)/shard_map/all_gather | solution.py:113
  505.4 486.5 %reduce-scatter.8.cloned.1.call-start = ((), (), s32[]{:S(2)}) async-start(), calls=%async_computation.7 | async-start | bytes 17301504 | tf_op jit(solution)/shard_map/reduce_scatter | solution.py:131
  519.6 253.2 %collective-permute-start.7 = (f32[256,2048]{1,0:T(8,128)}, f32[256,2048]{1,0:T(8,128)}, u32[]{:S(2)}, u32[]{:S(2)}) collective-permute-start(f32[256,2048]{1,0:T(8,128)} %get-tuple-element.99), channel_id=1, source_target_pairs={{4,0},{8,4},{12,8},{16,12},{20,16},{24,20},{28,24},{32,28},{36,32}... | collective-permute-start | bytes 6291464 | tf_op jit(solution)/shard_map/ppermute | solution.py:15
  520.9 251.9 %collective-permute-start.6 = (f32[256,2048]{1,0:T(8,128)}, f32[256,2048]{1,0:T(8,128)}, u32[]{:S(2)}, u32[]{:S(2)}) collective-permute-start(f32[256,2048]{1,0:T(8,128)} %get-tuple-element.98), channel_id=1, source_target_pairs={{8,0},{12,4},{16,8},{20,12},{24,16},{28,20},{32,24},{36,28},{40,32... | collective-permute-start | bytes 6291464 | tf_op jit(solution)/shard_map/ppermute | solution.py:15
  522.2 250.6 %collective-permute-start.5 = (f32[256,2048]{1,0:T(8,128)}, f32[256,2048]{1,0:T(8,128)}, u32[]{:S(2)}, u32[]{:S(2)}) collective-permute-start(f32[256,2048]{1,0:T(8,128)} %get-tuple-element.96), channel_id=1, source_target_pairs={{12,0},{16,4},{20,8},{24,12},{28,16},{32,20},{36,24},{40,28},{44,3... | collective-permute-start | bytes 6291464 | tf_op jit(solution)/shard_map/ppermute | solution.py:15
  523.5 3.8 copy-start.1
  525.9 25.9 %collective-permute-start.4 = (f32[128,2048]{1,0:T(8,128)}, f32[128,2048]{1,0:T(8,128)}, u32[]{:S(2)}, u32[]{:S(2)}) collective-permute-start(f32[128,2048]{1,0:T(8,128)} %fusion.13), channel_id=1, source_target_pairs={{16,0},{20,4},{24,8},{28,12},{32,16},{36,20},{40,24},{44,28},{48,3... | collective-permute-start | bytes 3145736 | tf_op jit(solution)/shard_map/ppermute | solution.py:15
Sparse Core Ops, SparseCore 0:
  18.4 198.8 reduce-scatter.3
  335.9 169.4 reduce-scatter.5
  507.1 261.4 all-gather.1
  770.9 220.8 reduce-scatter.7
